TPU v7x, 128 devices: a whole 4x4x4 slice. The times are simulated.
128 devices in a mesh: seq: 32 (over z, x, core), head: 4 (over y).
Axes of the slice: x: 4, y: 4, z: 4, core: 2. Of those that a mesh axis runs over, the one named last changes fastest.
Arguments:
- hidden: bfloat16 [8192, 2048], P('seq'), may hold values from -6 to 6
- w_query: bfloat16 [2048, 2048], P(None, 'head'), may hold values from -0.125 to 0.125
- w_key: bfloat16 [2048, 2048], P(None, 'head'), as said below
- w_value: bfloat16 [2048, 4096], P(None, 'head'), may hold values from -0.125 to 0.125
- w_gate: bfloat16 [2048, 4096], P(None, 'head'), may hold values from -0.125 to 0.125
- w_beta: bfloat16 [2048, 32], P(None, 'head'), may hold values from -0.125 to 0.125
- conv_query: bfloat16 [4, 2048], P(None, 'head'), may hold values from -3 to 3
- conv_key: bfloat16 [4, 2048], P(None, 'head'), may hold values from -3 to 3
- conv_value: bfloat16 [4, 4096], P(None, 'head'), may hold values from -3 to 3
- norm_gain: bfloat16 [128], replicated, may hold values from 0.5 to 1.5
- w_out: bfloat16 [4096, 2048], P('head'), may hold values from -0.09375 to 0.09375
Outputs:
- mixed: bfloat16 [8192, 2048], P('seq', 'head')
Inputs may be any that keep to these rules, and one draw needn't show every extreme that they name: `w_key`: entries of the key projection.
All inputs are finite; a program needn't handle non-finite values.
Results may differ from a plain program's by a relative error of at most 0.017.
Values may be sent and summed in bfloat16 or wider, within the bound.
A program may use at most 128 MiB of HBM per device.

v0:
```python
import functools

import jax
import jax.numpy as jnp
from jax import lax
from jax.experimental import pallas as pl
from jax.experimental.pallas import tpu as pltpu
from jax.sharding import PartitionSpec as P

DK = 128
DV = 128
KER = 4
HALO = 16
FILL = 2
eps_norm = 1e-06
F32 = jnp.float32
BF16 = jnp.bfloat16
MESH = pl.DeviceIdType.MESH


def mm(a, b):
    return jnp.dot(a, b, preferred_element_type=F32)


def mm_nt(a, b):
    return lax.dot_general(a, b, (((1,), (1,)), ((), ())), preferred_element_type=F32)


def mm_tn(a, b):
    return lax.dot_general(a, b, (((0,), (0,)), ((), ())), preferred_element_type=F32)


def sigmoid(x):
    return 0.5 + 0.5 * jnp.tanh(0.5 * x)


def silu(x):
    half = 0.5 * x
    return half + half * jnp.tanh(half)


def unit_rows(x):
    return x * lax.rsqrt(jnp.sum(x * x, axis=-1, keepdims=True) + eps_norm)


def block_solve(sys_ref, x_ref, fill):
    count, n = sys_ref.shape[:2]
    zero = jnp.zeros((), BF16)

    def indices():
        return (
            lax.broadcasted_iota(jnp.int32, (n, n), 0),
            lax.broadcasted_iota(jnp.int32, (n, n), 1),
        )

    def pick(i, size, first, stride):
        lane = lax.broadcasted_iota(jnp.int32, (size, n), 1) // size
        out = jnp.zeros((size, n), F32)
        for b in range(first, n // size, stride):
            out = jnp.where(lane == b - first, sys_ref[i, b * size : (b + 1) * size], out)
        return out

    def spread(x, size, mask):
        return jnp.where(mask, jnp.concatenate([x.astype(BF16)] * (n // size), axis=0), zero)

    def series():
        size = 16
        row, col = indices()
        same = (row // size) == (col // size)
        small = lax.broadcasted_iota(jnp.int32, (size, n), 1) % size
        eye = (small == lax.broadcasted_iota(jnp.int32, (size, n), 0)).astype(F32)
        powers = [-pick(i, size, 0, 1) for i in range(count)]
        solved = [eye + p for p in powers]
        powers = [mm(p.astype(BF16), spread(p, size, same)) for p in powers]
        for last in (False, False, True):
            wide = [spread(p, size, same) for p in powers]
            if last:
                solved = [x + mm(x.astype(BF16), w) for x, w in zip(solved, wide)]
            else:
                both = [
                    mm(jnp.concatenate([x, p], axis=0).astype(BF16), w)
                    for x, p, w in zip(solved, powers, wide)
                ]
                solved = [x + y[:size] for x, y in zip(solved, both)]
                powers = [y[size:] for y in both]
        for i in range(count):
            x_ref[i, :size] = solved[i]
        fill()

    series()
    size = 16
    while size < n:

        def double(size):
            row, col = indices()
            same = (row // size) == (col // size)
            below = ((row // size) == (col // size) + 1) & ((row // size) % 2 == 1)
            odd = (lax.broadcasted_iota(jnp.int32, (size, n), 1) // size) % 2 == 1
            solved = [x_ref[i, :size] for i in range(count)]
            cross = [
                mm(pick(i, size, 1, 2).astype(BF16), spread(x, size, same))
                for i, x in enumerate(solved)
            ]
            cross = [mm(x.astype(BF16), spread(c, size, below)) for x, c in zip(solved, cross)]
            for i in range(count):
                x_ref[i, :size] = jnp.where(odd, 0.0, solved[i])
                x_ref[i, size : 2 * size] = jnp.where(odd, solved[i], -cross[i])
            fill()

        double(size)
        size *= 2


def query_side(queries, kb):
    half = queries[0].shape[0] // 2
    row = lax.broadcasted_iota(jnp.int32, (half, half), 0)
    col = lax.broadcasted_iota(jnp.int32, (half, half), 1)
    masked = []
    for q, k in zip(queries, kb):
        score = mm_nt(q.astype(BF16), k)
        upper = jnp.where(row >= col, score[:half, :half], 0.0).astype(BF16)
        lower = jnp.concatenate(
            [score[half:, :half], jnp.where(row >= col, score[half:, half:], 0.0)], axis=1
        ).astype(BF16)
        masked.append((upper, lower))
    return masked


def value_side(solves, sides):
    half = sides[0].shape[0] // 2
    tops = [mm(x[0], s[:half].astype(BF16)).astype(BF16) for x, s in zip(solves, sides)]
    rest = [(s[half:] - mm(x[2], t)).astype(BF16) for s, x, t in zip(sides, solves, tops)]
    ends = [mm(x[1], r).astype(BF16) for x, r in zip(solves, rest)]
    return [jnp.concatenate(pair, axis=0) for pair in zip(tops, ends)]


def join(first, second):
    return first + second - mm(second[:, :DK].astype(BF16), first.astype(BF16))


def layer_kernel(
    sizes, hid, wq, wk, wv, wg, wb, cq, ck, cv, gain, wo, out_ref, bufs, rule, scan, shares
):
    size_seq, size_head, members = sizes
    groups = size_seq // members
    me, row_at = lax.axis_index("seq"), lax.axis_index("head")
    slot, team = lax.rem(me, members), me // members
    after, before = lax.rem(me + 1, size_seq), lax.rem(me + size_seq - 1, size_seq)
    peers = [team * members + lax.rem(slot + d, members) for d in range(1, members)]
    mates = [lax.rem(team + d, groups) * members + slot for d in range(1, groups)]
    others = [lax.rem(row_at + d, size_head) for d in range(1, size_head)]

    def remote(src, dst, send, recv, to):
        return pltpu.make_async_remote_copy(
            src_ref=src, dst_ref=dst, send_sem=send, recv_sem=recv, device_id=to, device_id_type=MESH
        )

    barrier = pltpu.get_barrier_semaphore()
    greeted = [{"seq": i} for i in [after, before] + peers + mates]
    greeted += [{"head": i} for i in (others[0], others[-1])]
    for to in greeted:
        pl.semaphore_signal(barrier, inc=1, device_id=to, device_id_type=MESH)

    h_buf, q_buf, k_buf, v_buf, g_buf, o_buf, halo, load_sem, edge_send, edge_recv = bufs
    rows = h_buf.shape[0]
    ways = ((hid, h_buf), (wk, k_buf), (wq, q_buf), (wv, v_buf), (wg, g_buf), (wo, o_buf))
    loads = [pltpu.make_async_copy(src, dst, load_sem.at[i]) for i, (src, dst) in enumerate(ways)]
    load_h, load_k, load_q, load_v, load_g, load_o = loads
    for copy in loads[:-2]:
        copy.start()

    pl.semaphore_wait(barrier, len(greeted))

    edge = remote(hid.at[pl.ds(rows - HALO, HALO)], halo, edge_send, edge_recv, {"seq": after})
    edge.start()

    ext_v, ext_k, ext_q, part_ref, ask_ref, carry_ref = rule[:6]
    sys_ref, x_ref, key_ref, beta_ref, corner_ref, side_ref = rule[6:]
    load_h.wait()
    h = h_buf[...]
    beta = 0.05 + 0.15 * sigmoid(mm_nt(h, wb[...]))
    heads = beta.shape[1]
    lane = lax.broadcasted_iota(jnp.int32, (heads, heads * DK), 1) // DK
    ones = (lane == lax.broadcasted_iota(jnp.int32, (heads, heads * DK), 0)).astype(F32).astype(BF16)
    top = beta.astype(BF16)
    beta_ref[...] = mm(top, ones) + mm((beta - top.astype(F32)).astype(BF16), ones)

    def taps_over(x, t):
        summed = t[KER - 1 :] * x
        for n in range(KER - 1):
            summed = summed + t[n : n + 1] * pltpu.roll(x, KER - 1 - n, 0)
        return summed

    def convolve(ext, edge_rows, taps, j):
        at = slice(j * DK, (j + 1) * DK)
        t = 0.5 * taps[:, at].astype(F32)
        body = taps_over(ext[:, at], t)
        brink = jnp.concatenate([edge_rows[:, at], ext[:8, at]], axis=0)
        summed = jnp.concatenate([taps_over(brink, t)[8:], body[8:]], axis=0)
        return summed + summed * jnp.tanh(summed)

    projections = ((load_k, k_buf, ext_k), (load_q, q_buf, ext_q), (load_v, v_buf, ext_v))
    for load, w, ext in projections:
        load.wait()
        ext[...] = mm(h, w[...])
    load_g.start()
    load_o.start()
    edge.wait_recv()
    border = halo[...]
    border = jnp.where(me > 0, border, jnp.zeros_like(border))
    edge_k, edge_q, edge_v = [mm(border, w[...])[HALO - 8 :] for _, w, _ in projections]
    count = k_buf.shape[1] // DK
    group = heads // count
    half = rows // 2
    keys = [unit_rows(convolve(ext_k, edge_k, ck, j)) for j in range(count)]
    kb = [k.astype(BF16) for k in keys]
    row = lax.broadcasted_iota(jnp.int32, (half, half), 0)
    col = lax.broadcasted_iota(jnp.int32, (half, half), 1)
    for n, k in enumerate(kb):
        gram = mm_nt(k, k)
        first = jnp.where(row > col, gram[:half, :half], 0.0)
        last = jnp.where(row > col, gram[half:, half:], 0.0)
        key_ref[n] = keys[n]
        for j in range(n * group, (n + 1) * group):
            b = beta_ref[:, j * DK : (j + 1) * DK]
            sys_ref[2 * j] = b[:half] * first
            sys_ref[2 * j + 1] = b[half:] * last
            corner_ref[j] = (b[half:] * gram[half:, :half]).astype(BF16)
    done = []

    def fill():
        for j in range(len(done), min(len(done) + FILL, heads)):
            b = beta_ref[:, j * DK : (j + 1) * DK]
            side_ref[j, :, :DK] = b * key_ref[j // group]
            side_ref[j, :, DK:] = b * convolve(ext_v, edge_v, cv, j)
            done.append(j)

    block_solve(sys_ref, x_ref, fill)
    while len(done) < heads:
        fill()
    solves = [
        (x_ref[2 * j].astype(BF16), x_ref[2 * j + 1].astype(BF16), corner_ref[j])
        for j in range(heads)
    ]
    sides = [side_ref[j] for j in range(heads)]

    got, total, total_got, start, state_ref, s1, r1, s2, r2, s3, r3 = scan

    turns = [(n * members // 4, c) for n in (0, 1, 3, 2) for c in range(members // 4)]
    near = [
        lax.rem(slot - lax.rem(slot, members // 4) + n, members) + lax.rem(slot + c, members // 4)
        for n, c in turns
    ]

    def to_member(src, dst, send, recv, d):
        return remote(
            src.at[near[d]], dst.at[slot], send.at[d], recv.at[slot], {"seq": team * members + near[d]}
        )

    sends = []
    sides = value_side(solves, sides)
    for j, side in enumerate(sides):
        carry_ref[j] = mm_tn(kb[j // group], side).astype(BF16)
    for d in reversed(range(1, members)):
        copy = to_member(carry_ref, got, s1, r1, d)
        copy.start()
        sends.append(copy)
    got[slot] = carry_ref[slot]

    queries = [unit_rows(convolve(ext_q, edge_q, cq, j)) for j in range(count)]
    masked = query_side(queries, kb)
    for j, side in enumerate(sides):
        at = slice(j * DV, (j + 1) * DV)
        upper, lower = masked[j // group]
        seen = jnp.concatenate([mm(upper, side[:half]), mm(lower, side)], axis=0)
        part_ref[:, at] = seen[:, DK:]
        ask_ref[:, at] = (queries[j // group] - seen[:, :DK]).astype(BF16)
    gate_ref, gated_ref, keep, relay, opp, direct, hop, land, sr, rr = shares
    load_g.wait()
    gain_row = gain[...].astype(F32)
    gate = silu(mm(h, g_buf[...]).astype(BF16).astype(F32))
    for j in range(heads):
        at = slice(j * DV, (j + 1) * DV)
        gate_ref[:, at] = gate[:, at] * gain_row

    spans = []
    for i in range(members):

        @pl.when(slot != i)
        def _():
            remote(got.at[i], got.at[i], s1.at[0], r1.at[i], {"seq": peers[0]}).wait_recv()

        spans.append(got[i].astype(F32))
    level = {(i, i + 1): x for i, x in enumerate(spans)}
    size = 1
    while size < members:
        for i in range(0, members, 2 * size):
            level[i, i + 2 * size] = join(level[i, i + size], level[i + size, i + 2 * size])
        size *= 2
    total[...] = level[0, members].astype(BF16)
    late = pl.ds(DK, DV)

    def to_mate(d, part):
        return remote(
            total.at[:, part], total_got.at[team, :, part], s2.at[d], r2.at[team], {"seq": mates[d - 1]}
        )

    def each_mate(act):
        for d in sorted(range(1, groups), key=lambda d: -min(d, groups - d)):
            pl.when(team == 0)(lambda: act(to_mate(d, late)))
            pl.when((team > 0) & (team + d < groups))(lambda: act(to_mate(d, pl.ds(0, DK + DV))))

    each_mate(lambda copy: copy.start())

    prefix = [None]
    for i in range(1, members):
        size = i & -i
        if i > size:
            level[0, i] = join(level[0, i - size], level[i - size, i])
        prefix.append(level[0, i])
    state = jnp.zeros((DK, DV), F32)
    for i in range(groups - 1):

        @pl.when(team > i)
        def _():
            part = total_got.at[i, :, late] if i == 0 else total_got.at[i]
            remote(part, part, s2.at[0], r2.at[i], {"seq": mates[0]}).wait_recv()

        whole = total_got[i].astype(F32)
        moved = whole[:, DK:]
        if i > 0:
            moved = moved + state - mm(whole[:, :DK].astype(BF16), state.astype(BF16))
        state = jnp.where(team > i, moved, state)
    entry = state
    rounded = entry.astype(BF16)
    start[0] = rounded
    for i in range(1, members):
        begin = entry + prefix[i][:, DK:] - mm(prefix[i][:, :DK].astype(BF16), rounded)
        start[i] = begin.astype(BF16)
    for d in reversed(range(1, members)):
        copy = to_member(start, state_ref, s3, r3, d)
        copy.start()
        sends.append(copy)
    state_ref[slot] = start[slot]
    for d in range(0, members, 2):
        for i in near[max(d, 1) : d + 2]:
            remote(state_ref.at[i], state_ref.at[i], s3.at[0], r3.at[i], {"seq": peers[0]}).wait_recv()
        at = [pl.ds(pl.multiple_of(i * DV, DV), DV) for i in near[d : d + 2]]
        pair = [part_ref[:, c] + mm(ask_ref[:, c], state_ref[i]) for c, i in zip(at, near[d : d + 2])]
        scales = [lax.rsqrt(jnp.mean(x * x, axis=-1, keepdims=True) + eps_norm) for x in pair]
        for c, x, scale in zip(at, pair, scales):
            gated_ref[:, c] = (x * scale * gate_ref[:, c]).astype(BF16)

    load_o.wait()
    gated = gated_ref[...]
    tile = out_ref.shape[1]
    half = rows // 2
    upper, lower = pl.ds(0, half), pl.ds(half, half)

    def share(to):
        columns = pl.ds(pl.multiple_of(to * tile, tile), tile)
        return mm(gated, o_buf[:, columns]).astype(BF16)

    right, far, left = others
    opp[...] = share(far)
    hops = [
        remote(opp.at[upper], hop.at[upper], sr.at[0], rr.at[0], {"head": right}),
        remote(opp.at[lower], hop.at[lower], sr.at[1], rr.at[1], {"head": left}),
    ]
    for copy in hops:
        copy.start()
    to_right, to_left = share(right), share(left)
    keep[upper], keep[lower] = to_right[:half], to_left[half:]
    direct[lower], direct[upper] = to_right[half:], to_left[:half]
    lands = [
        remote(direct.at[lower], land.at[lower], sr.at[2], rr.at[2], {"head": right}),
        remote(direct.at[upper], land.at[upper], sr.at[3], rr.at[3], {"head": left}),
    ]
    for copy in lands:
        copy.start()
    ends = []
    for n, (at, to) in enumerate(((upper, right), (lower, left))):
        hops[n].wait_recv()
        relay[at] = (hop[at].astype(F32) + keep[at].astype(F32)).astype(BF16)
        copy = remote(relay.at[at], hop.at[pl.ds(rows + n * half, half)], sr.at[4 + n], rr.at[4 + n], {"head": to})
        copy.start()
        ends.append(copy)
    mine = share(row_at).astype(F32)
    for n, at in ((1, upper), (0, lower)):
        lands[n].wait_recv()
        ends[1 - n].wait_recv()
        top = 0 if n == 1 else half
        out_ref[at] = (
            mine[top : top + half] + land[at].astype(F32) + hop[pl.ds(rows + top, half)].astype(F32)
        ).astype(BF16)

    edge.wait_send()
    for copy in sends + hops + lands + ends:
        copy.wait_send()
    each_mate(lambda copy: copy.wait_send())


def shards(
    hidden,
    w_query,
    w_key,
    w_value,
    w_gate,
    w_beta,
    conv_query,
    conv_key,
    conv_value,
    norm_gain,
    w_out,
):
    size_seq, size_head = lax.axis_size("seq"), lax.axis_size("head")
    rows, depth = hidden.shape
    wide = w_value.shape[1]
    heads = wide // DV
    groups = size_seq // heads
    tile = w_out.shape[1] // size_head
    vmem = pl.BlockSpec(memory_space=pltpu.VMEM)
    hbm = pl.BlockSpec(memory_space=pl.ANY)
    like = lambda a: pltpu.VMEM(a.shape, a.dtype)
    dma = pltpu.SemaphoreType.DMA
    bufs = [like(a) for a in (hidden, w_query, w_key, w_value, w_gate, w_out)]
    bufs += [pltpu.VMEM((HALO, depth), BF16), dma((6,)), dma, dma]
    rule = [
        pltpu.VMEM((rows, wide), F32),
        pltpu.VMEM((rows, w_key.shape[1]), F32),
        pltpu.VMEM((rows, w_query.shape[1]), F32),
        pltpu.VMEM((rows, wide), F32),
        pltpu.VMEM((rows, wide), BF16),
        pltpu.VMEM((heads, DK, DK + DV), BF16),
        pltpu.VMEM((2 * heads, rows // 2, rows // 2), F32),
        pltpu.VMEM((2 * heads, rows // 2, rows // 2), F32),
        pltpu.VMEM((w_key.shape[1] // DK, rows, DK), F32),
        pltpu.VMEM((rows, heads * DK), F32),
        pltpu.VMEM((heads, rows // 2, rows // 2), BF16),
        pltpu.VMEM((heads, rows, DK + DV), F32),
    ]
    scan = [
        pltpu.VMEM((heads, DK, DK + DV), BF16),
        pltpu.VMEM((DK, DK + DV), BF16),
        pltpu.VMEM((groups, DK, DK + DV), BF16),
        pltpu.VMEM((heads, DK, DV), BF16),
        pltpu.VMEM((heads, DK, DV), BF16),
    ]
    scan += [dma((heads,)), dma((heads,)), dma((groups,)), dma((groups,)), dma((heads,)), dma((heads,))]
    shares = [pltpu.VMEM((rows, wide), F32), pltpu.VMEM((rows, wide), BF16)]
    shares += [pltpu.VMEM((rows, tile), BF16)] * 4
    shares += [pltpu.VMEM((2 * rows, tile), BF16), pltpu.VMEM((rows, tile), BF16), dma((6,)), dma((6,))]
    return pl.pallas_call(
        functools.partial(layer_kernel, (size_seq, size_head, heads)),
        in_specs=[hbm] * 5 + [vmem] * 5 + [hbm],
        out_specs=vmem,
        out_shape=pltpu.VMEM((rows, tile), BF16),
        scratch_shapes=[bufs, rule, scan, shares],
        compiler_params=pltpu.CompilerParams(collective_id=0, has_side_effects=True),
        name="layer",
    )(
        hidden,
        w_query,
        w_key,
        w_value,
        w_gate,
        w_beta.T,
        conv_query,
        conv_key,
        conv_value,
        norm_gain.reshape(1, DV),
        w_out,
    )


def solution(mesh):
    in_specs = (
        P("seq", None),
        P(None, "head"),
        P(None, "head"),
        P(None, "head"),
        P(None, "head"),
        P(None, "head"),
        P(None, "head"),
        P(None, "head"),
        P(None, "head"),
        P(),
        P("head", None),
    )
    out_specs = P("seq", "head")
    return jax.shard_map(shards, mesh=mesh, in_specs=in_specs, out_specs=out_specs, check_vma=False)
```

profile of v0, /device:TPU:64, one launch (start us, length us, event | category | flops | bytes accessed | tf_op | source)
XLA Modules:
  0.0 42.3 jit_solution(12346988252164361302)
XLA Ops:
  0.0 41.6 %layer.1 = bf16[256,512]{1,0:T(8,128)(2,1)S(1)} custom-call(bf16[256,2048]{1,0:T(8,128)(2,1)} %hid.1, bf16[2048,512]{1,0:T(8,128)(2,1)} %wq.1, bf16[2048,512]{1,0:T(8,128)(2,1)} %wk.1, bf16[2048,1024]{1,0:T(8,128)(2,1)} %wv.1, bf16[2048,1024]{1,0:T(8,128)(2,1)} %wg.1, bf16[8,2048]{1,0:T(8,128)(2,1)} %bitcast.2, bf16[4,512]{1,0:T(4,128)(2,1)} %cq.1, ...), custom_call_target="tpu_custom_call" | custom-call | tf_op jit(solution)/shard_map/layer/pallas_call | solution.py:453
  41.6 0.7 %copy.13 = bf16[256,512]{1,0:T(8,128)(2,1)} copy(bf16[256,512]{1,0:T(8,128)(2,1)S(1)} %layer.1) | data formatting | bytes 524288
where the time goes:
time: 43.1 us; the launch traced here: 42.3 us
  Pallas kernels  41.6 us (97%)
  local copies, waits for them, and re-layouts  0.71 us (2%)
    pallas_call x1, Pallas kernels, shards(): pl.pallas_call(functools.partial(layer_kernel, (size_seq, size_head, head...  41.6 us

commit v1 on v0

--- a/solution.py
+++ b/solution.py
@@ -10,7 +10,7 @@
 DK = 128
 DV = 128
 KER = 4
-HALO = 16
+HALO = 8
 FILL = 2
 eps_norm = 1e-06
 F32 = jnp.float32
@@ -276,13 +276,6 @@
         part_ref[:, at] = seen[:, DK:]
         ask_ref[:, at] = (queries[j // group] - seen[:, :DK]).astype(BF16)
     gate_ref, gated_ref, keep, relay, opp, direct, hop, land, sr, rr = shares
-    load_g.wait()
-    gain_row = gain[...].astype(F32)
-    gate = silu(mm(h, g_buf[...]).astype(BF16).astype(F32))
-    for j in range(heads):
-        at = slice(j * DV, (j + 1) * DV)
-        gate_ref[:, at] = gate[:, at] * gain_row
-
     spans = []
     for i in range(members):
 
@@ -311,6 +304,13 @@
             pl.when((team > 0) & (team + d < groups))(lambda: act(to_mate(d, pl.ds(0, DK + DV))))
 
     each_mate(lambda copy: copy.start())
+
+    load_g.wait()
+    gain_row = gain[...].astype(F32)
+    gate = silu(mm(h, g_buf[...]).astype(BF16).astype(F32))
+    for j in range(heads):
+        at = slice(j * DV, (j + 1) * DV)
+        gate_ref[:, at] = gate[:, at] * gain_row
 
     prefix = [None]
     for i in range(1, members):

time: 43.1 us -> 43.1 us (level)
  no operation moved by 1% of the time
where the time goes in v1:
time: 43.1 us; the launch traced here: 42.2 us
  Pallas kernels  41.5 us (96%)
  local copies, waits for them, and re-layouts  0.71 us (2%)
    pallas_call x1, Pallas kernels, shards(): pl.pallas_call(functools.partial(layer_kernel, (size_seq, size_head, head...  41.5 us

profile of v1, /device:TPU:64, one launch (start us, length us, event | category | flops | bytes accessed | tf_op | source)
XLA Modules:
  0.0 42.2 jit_solution(3264002408181596009)
XLA Ops:
  0.0 41.5 %layer.1 = bf16[256,512]{1,0:T(8,128)(2,1)S(1)} custom-call(bf16[256,2048]{1,0:T(8,128)(2,1)} %hid.1, bf16[2048,512]{1,0:T(8,128)(2,1)} %wq.1, bf16[2048,512]{1,0:T(8,128)(2,1)} %wk.1, bf16[2048,1024]{1,0:T(8,128)(2,1)} %wv.1, bf16[2048,1024]{1,0:T(8,128)(2,1)} %wg.1, bf16[8,2048]{1,0:T(8,128)(2,1)} %bitcast.2, bf16[4,512]{1,0:T(4,128)(2,1)} %cq.1, ...), custom_call_target="tpu_custom_call" | custom-call | tf_op jit(solution)/shard_map/layer/pallas_call | solution.py:453
  41.5 0.7 %copy.13 = bf16[256,512]{1,0:T(8,128)(2,1)} copy(bf16[256,512]{1,0:T(8,128)(2,1)S(1)} %layer.1) | data formatting | bytes 524288
